TPU v7x, 128 devices: a whole 4x4x4 slice. The times are simulated.
128 devices in a mesh: seq: 8 (over x, core), grp: 16 (over z, y).
Axes of the slice: x: 4, y: 4, z: 4, core: 2. Of those that a mesh axis runs over, the one named last changes fastest.
Arguments:
- tokens: bfloat16 [16, 1024, 1536], P('grp', 'seq'), may hold values from -15 to 15
- lengths: int32 [16, 3], P('grp'), may hold values from 1 to 512, 1024 in all within a row
- prompt_adapter: int32 [16, 3], P('grp'), may hold values from 0 to 15
- routes: int32 [16, 1024, 8], P('grp', 'seq'), may hold values from 0 to 39, all different within a row; in each aligned block of 128 rows (0 to 127, 128 to 255, ..., all dimensions but the last counted through in order) at most 40 rows name the same one
- routing_weight: float32 [16, 1024, 8], P('grp', 'seq'), may hold values from 0.1 to 1
- attention_gain: float32 [1536], replicated, may hold values from 0.5 to 1.5
- query_weight: bfloat16 [1536, 1536], replicated, may hold values from -25 to 25
- key_weight: bfloat16 [1536, 512], replicated, may hold values from -0.15625 to 0.15625
- value_weight: bfloat16 [1536, 512], replicated, may hold values from -0.15625 to 0.15625
- output_weight: bfloat16 [1536, 1536], replicated, may hold values from -0.15625 to 0.15625
- adapter_down_maps: bfloat16 [4, 16, 1536, 16], P(None, 'grp'), may hold values from -0.15625 to 0.15625
- adapter_up_query_output: bfloat16 [2, 16, 16, 1536], P(None, 'grp'), may hold values from -1.5 to 1.5
- adapter_up_key_value: bfloat16 [2, 16, 16, 512], P(None, 'grp'), may hold values from -1.5 to 1.5
- expert_gain: float32 [1536], replicated, may hold values from 0.5 to 1.5
- gate_weight: bfloat16 [80, 1536, 256], P('grp'), may hold values from -0.15625 to 0.15625
- up_weight: bfloat16 [80, 1536, 256], P('grp'), may hold values from -0.15625 to 0.15625
- down_weight: bfloat16 [80, 256, 1536], P('grp'), may hold values from -0.25 to 0.25
- closing_gain: float32 [1536], replicated, may hold values from 0.5 to 1.5
- vocab_projection: bfloat16 [1536, 49152], P(None, ('seq', 'grp')), may hold values from -10 to 10
Outputs:
- hidden_out: bfloat16 [16, 1024, 1536], P('grp', 'seq')
- log_probs: float32 [48, 49152], P(None, ('seq', 'grp'))
Inputs may be any that keep to these rules, and one draw needn't show every extreme that they name: The 3 lengths of a group sum to 1024; the longest is exactly 512. `routes`: A token names 8 different experts. Within the 128 tokens of one device no expert is named by more than 40 of them, and in every draw some expert is named by exactly 40 tokens of some device.
All inputs are finite; a program needn't handle non-finite values.
Results may differ from a plain program's by a relative error of at most 0.017.
The roundings to bfloat16 on the way count: a program that leaves them out, or rounds other values in their place, can miss the bound.
Values may be sent and summed in bfloat16 or wider, within the bound.
No kernel may reach another device: no remote copies, remote signals or barrier semaphores. Data moves between devices by JAX's collectives and lax.ppermute only.
A program may use at most 192 MiB of HBM per device.

v0:
```python
import jax
import jax.numpy as jnp
from jax import lax
from jax.sharding import PartitionSpec as P

HEADS = 24
KV_HEADS = 8
HEAD = 64
EXPERTS = 40
TOP = 8
CAP = 40
EPSILON = 1e-05
ROPE_BASE = 10000.0
MASKED = -1e30


def rms_scaled(features, scales):
    features = features.astype(jnp.float32)
    inverse = lax.rsqrt(jnp.mean(features * features, axis=-1, keepdims=True) + EPSILON)
    return (features * inverse * scales).astype(jnp.bfloat16)


def rotate(features, offsets):
    half_size = features.shape[-1] // 2
    frequency = ROPE_BASE ** (-jnp.arange(half_size, dtype=jnp.float32) / half_size)
    angles = offsets.astype(jnp.float32)[:, None, None] * frequency[None, None, :]
    cosine = jnp.cos(angles)
    sines = jnp.sin(angles)
    first_half = features[..., :half_size]
    second = features[..., half_size:]
    return jnp.concatenate(
        [first_half * cosine - second * sines, second * cosine + first_half * sines], axis=-1
    )


def doc_layout(prompt_lens, row_index):
    doc_ends = jnp.cumsum(prompt_lens)
    starts = doc_ends - prompt_lens
    document = jnp.sum((row_index[:, None] >= doc_ends[None, :]).astype(jnp.int32), axis=1)
    member = document[:, None] == jnp.arange(prompt_lens.shape[0], dtype=jnp.int32)[None, :]
    doc_start = jnp.sum(jnp.where(member, starts[None, :], 0), axis=1)
    return (document, row_index - doc_start, member)


def adapter_delta(normalized_rows, selected_experts, down_proj, up_weights):
    low_rank = jnp.einsum(
        "td,adr->tar", normalized_rows, down_proj, preferred_element_type=jnp.float32
    )
    low_rank = (low_rank * selected_experts[:, :, None]).astype(jnp.bfloat16)
    return jnp.einsum("tar,are->te", low_rank, up_weights, preferred_element_type=jnp.float32)


def body(
    tokens,
    lengths,
    prompt_adapter,
    routes,
    routing_weight,
    attention_gain,
    query_weight,
    key_weight,
    value_weight,
    output_weight,
    adapter_down_maps,
    adapter_up_query_output,
    adapter_up_key_value,
    expert_gain,
    gate_weight,
    up_weight,
    down_weight,
    closing_gain,
    vocab_projection,
):
    rows_in = tokens[0]
    tok_count = rows_in.shape[0]
    model_width = rows_in.shape[1]
    prompt_lens = lengths[0]
    owners = prompt_adapter[0]
    ratio = HEADS // KV_HEADS
    logit_scale = HEAD ** (-0.5)
    down_all, wide_all, narrow_all = (
        lax.all_gather(adapter_down_maps, "grp", axis=1, tiled=True),
        lax.all_gather(adapter_up_query_output, "grp", axis=1, tiled=True),
        lax.all_gather(adapter_up_key_value, "grp", axis=1, tiled=True),
    )
    row_index = lax.axis_index("seq") * tok_count + jnp.arange(tok_count, dtype=jnp.int32)
    document, offsets, member = doc_layout(prompt_lens, row_index)
    adapter = jnp.sum(jnp.where(member, owners[None, :], 0), axis=1)
    selected_experts = (
        adapter[:, None] == jnp.arange(down_all.shape[1], dtype=jnp.int32)[None, :]
    ).astype(jnp.float32)
    normalized_rows = rms_scaled(rows_in, attention_gain)
    query_matrix = jnp.dot(
        normalized_rows, query_weight, preferred_element_type=jnp.float32
    ) + adapter_delta(normalized_rows, selected_experts, down_all[0], wide_all[0])
    query_matrix = rotate(query_matrix.reshape(tok_count, HEADS, HEAD), offsets).astype(
        jnp.bfloat16
    )
    query_matrix = query_matrix.reshape(tok_count, KV_HEADS, ratio, HEAD)
    key_matrix = jnp.dot(
        normalized_rows, key_weight, preferred_element_type=jnp.float32
    ) + adapter_delta(normalized_rows, selected_experts, down_all[1], narrow_all[0])
    key_matrix = (
        rotate(key_matrix.reshape(tok_count, KV_HEADS, HEAD), offsets)
        .astype(jnp.bfloat16)
        .reshape(tok_count, KV_HEADS * HEAD)
    )
    value_matrix = (
        jnp.dot(normalized_rows, value_weight, preferred_element_type=jnp.float32)
        + adapter_delta(normalized_rows, selected_experts, down_all[2], narrow_all[1])
    ).astype(jnp.bfloat16)
    running_max = jnp.full((KV_HEADS, ratio, tok_count), MASKED, jnp.float32)
    key_part = lax.all_gather(key_matrix, "seq", axis=0, tiled=True)
    value_part = lax.all_gather(value_matrix, "seq", axis=0, tiled=True)
    key_count = key_part.shape[0]
    key_index = jnp.arange(key_count, dtype=jnp.int32)
    key_doc, _, _ = doc_layout(prompt_lens, key_index)
    allowed = (key_doc[None, :] == document[:, None]) & (key_index[None, :] <= row_index[:, None])
    attention_logits = (
        jnp.einsum(
            "jhlv,phv->hljp",
            query_matrix,
            key_part.reshape(key_count, KV_HEADS, HEAD),
            preferred_element_type=jnp.float32,
        )
        * logit_scale
    )
    attention_logits = jnp.where(allowed[None, None], attention_logits, MASKED)
    new_max = jnp.maximum(running_max, jnp.max(attention_logits, axis=-1))
    weights = jnp.where(allowed[None, None], jnp.exp(attention_logits - new_max[..., None]), 0.0)
    running_sum = jnp.sum(weights, axis=-1)
    weighted_values = jnp.einsum(
        "ukoe,euh->ukoh",
        weights.astype(jnp.bfloat16),
        value_part.reshape(key_count, KV_HEADS, HEAD),
        preferred_element_type=jnp.float32,
    )
    running_max, running_sum, weighted_values = (new_max, running_sum, weighted_values)
    attention_output = (
        (weighted_values / running_sum[..., None])
        .transpose(2, 0, 1, 3)
        .reshape(tok_count, HEADS * HEAD)
        .astype(jnp.bfloat16)
    )
    outside_mask = jnp.dot(
        attention_output, output_weight, preferred_element_type=jnp.float32
    ) + adapter_delta(attention_output, selected_experts, down_all[3], wide_all[1])
    mixed_rows = (rows_in.astype(jnp.float32) + outside_mask).astype(jnp.bfloat16)
    moe_in = rms_scaled(mixed_rows, expert_gain)
    expert_ids = routes[0].reshape(-1)
    flat_weights = routing_weight[0].reshape(-1)
    onehot = (expert_ids[:, None] == jnp.arange(EXPERTS, dtype=jnp.int32)[None, :]).astype(
        jnp.int32
    )
    slot_index = jnp.sum((jnp.cumsum(onehot, axis=0) - onehot) * onehot, axis=1)
    source_row = jnp.arange(expert_ids.shape[0], dtype=jnp.int32) // TOP
    slot_table = (
        jnp.full((EXPERTS * CAP,), tok_count, jnp.int32)
        .at[expert_ids * CAP + slot_index]
        .set(source_row)
        .reshape(EXPERTS, CAP)
    )
    padded = jnp.concatenate([moe_in, jnp.zeros((1, model_width), jnp.bfloat16)], axis=0)
    groups = lax.axis_size("grp")
    slices_here = gate_weight.shape[0]
    outgoing = padded[jnp.repeat(slot_table, 2, axis=0)].reshape(
        groups, slices_here, CAP, model_width
    )
    arrived = lax.all_to_all(outgoing, "grp", split_axis=0, concat_axis=0, tiled=True)
    gate_proj = jnp.einsum(
        "nlcd,ldf->nlcf", arrived, gate_weight, preferred_element_type=jnp.float32
    )
    up_proj = jnp.einsum("nlcd,ldf->nlcf", arrived, up_weight, preferred_element_type=jnp.float32)
    hidden = (jax.nn.silu(gate_proj) * up_proj).astype(jnp.bfloat16)
    halves = jnp.einsum(
        "nlcf,lfd->nlcd", hidden, down_weight, preferred_element_type=jnp.float32
    ).astype(jnp.bfloat16)
    returned = lax.all_to_all(halves, "grp", split_axis=0, concat_axis=0, tiled=True).reshape(
        -1, model_width
    )
    slice_ids = 2 * expert_ids[:, None] + jnp.arange(2, dtype=jnp.int32)[None, :]
    pick_index = slice_ids * CAP + slot_index[:, None]
    picked = returned[pick_index].astype(jnp.float32).reshape(tok_count, TOP * 2, model_width)
    holder = slice_ids // slices_here
    holder_hot = (holder[:, :, None] == jnp.arange(groups, dtype=jnp.int32)[None, None, :]).astype(
        jnp.float32
    )
    holder_hot = (holder_hot * flat_weights[:, None, None]).reshape(tok_count, TOP * 2, groups)
    partial_value = jnp.einsum(
        "tkg,tkd->tgd", holder_hot, picked, precision=lax.Precision.HIGHEST
    ).astype(jnp.bfloat16)
    combined = jnp.sum(partial_value.astype(jnp.float32), axis=1)
    hidden_out = (mixed_rows.astype(jnp.float32) + combined).astype(jnp.bfloat16)
    last_index = jnp.cumsum(prompt_lens) - 1
    selector = (last_index[:, None] == row_index[None, :]).astype(jnp.bfloat16)
    last_rows = jnp.dot(selector, hidden_out, preferred_element_type=jnp.float32)
    last_rows = rms_scaled(last_rows, closing_gain).astype(jnp.float32)
    own_group = (jnp.arange(groups, dtype=jnp.int32) == lax.axis_index("grp")).astype(jnp.float32)
    spread = own_group[:, None, None] * last_rows[None, :, :]
    gathered = lax.psum(spread, ("seq", "grp"))
    final_rows = gathered.reshape(-1, model_width).astype(jnp.bfloat16)
    logits = jnp.dot(final_rows, vocab_projection, preferred_element_type=jnp.float32)
    global_max = lax.pmax(jnp.max(logits, axis=1), ("seq", "grp"))
    global_sum = lax.psum(jnp.sum(jnp.exp(logits - global_max[:, None]), axis=1), ("seq", "grp"))
    log_probs = logits - (global_max + jnp.log(global_sum))[:, None]
    return (hidden_out[None], log_probs)


def solution(mesh):
    placed = (
        P("grp", "seq", None),
        P("grp", None),
        P("grp", None),
        P("grp", "seq", None),
        P("grp", "seq", None),
        P(),
        P(),
        P(),
        P(),
        P(),
        P(None, "grp", None, None),
        P(None, "grp", None, None),
        P(None, "grp", None, None),
        P(),
        P("grp", None, None),
        P("grp", None, None),
        P("grp", None, None),
        P(),
        P(None, ("seq", "grp")),
    )
    return jax.shard_map(
        body,
        mesh=mesh,
        in_specs=placed,
        out_specs=(P("grp", "seq", None), P(None, ("seq", "grp"))),
        check_vma=False,
    )
```

profile of v0, /device:TPU:1, one launch (start us, length us, event | category | flops | bytes accessed | tf_op | source)
XLA Modules:
  0.0 710.5 jit_solution(9158568903717004309)
XLA Ops:
  12.1 22.3 %all_gather.16 = bf16[2,16,16,512]{3,2,1,0:T(8,128)(2,1)S(1)} all-gather(bf16[2,1,16,512]{3,2,1,0:T(8,128)(2,1)} %param.31), channel_id=1, replica_groups=mesh['seq'=8,'grp'=16] {'grp'}, dimensions={1}, use_global_device_ids=true | all-gather | bytes 557056 | tf_op jit(solution)/shard_map/all_gather | solution.py:84
  34.4 11.3 %reduce-window.11 = s32[40,8,128]{2,1,0:T(8,128)S(1)} reduce-window(s32[40,8,128]{2,1,0:T(8,128)S(1)} %fusion.60, s32[]{:T(128)} %constant.32.clone.1), window={size=1x1x128 pad=0_0x0_0x127_0}, to_apply=%region_9.10 | reduce-window | flops 5201920 | bytes 327684 | tf_op jit(solution)/shard_map/reduce-window.1
  46.4 4.3 scatter_custom_fusion
  53.3 8.4 %all-gather.5.cloned.1.call-done = bf16[4,16,1536,16]{2,3,1,0:T(8,128)(2,1)} async-done(((bf16[4,1,1536,16]{2,3,1,0:T(8,128)(2,1)}), bf16[4,16,1536,16]{2,3,1,0:T(8,128)(2,1)}) %all-gather.5.cloned.1.call-update) | async-done | bytes 3145744 | tf_op jit(solution)/shard_map/all_gather | solution.py:82
  61.7 3.2 fusion.93
  70.3 35.7 %all-gather.9.cloned.1.call-done = bf16[2,16,16,1536]{3,2,1,0:T(8,128)(2,1)} async-done(((bf16[2,1,16,1536]{3,2,1,0:T(8,128)(2,1)}), bf16[2,16,16,1536]{3,2,1,0:T(8,128)(2,1)}) %all-gather.9.cloned.1.call-update) | async-done | bytes 1572880 | tf_op jit(solution)/shard_map/all_gather | solution.py:83
  115.3 16.3 %all-gather.7.cloned.1.call-done = bf16[1024,512]{0,1:T(8,128)(2,1)} async-done(((bf16[128,512]{0,1:T(8,128)(2,1)}), bf16[1024,512]{0,1:T(8,128)(2,1)}) %all-gather.7.cloned.1.call-update) | async-done | bytes 1048592 | tf_op jit(solution)/shard_map/all_gather | solution.py:113
  134.8 4.5 copy-done.2
  142.4 15.8 %all-gather.11.cloned.1.call-done = bf16[1024,512]{1,0:T(8,128)(2,1)} async-done(((bf16[128,512]{1,0:T(8,128)(2,1)}), bf16[1024,512]{1,0:T(8,128)(2,1)}) %all-gather.11.cloned.1.call-update) | async-done | bytes 1048592 | tf_op jit(solution)/shard_map/all_gather | solution.py:114
  160.5 8.1 %fusion.40 = bf16[128,8,3,64]{0,3,2,1:T(8,128)(2,1)S(1)} fusion(bf16[1024,8,64,1]{0,2,3,1:T(8,128)(2,1)} %bitcast.215, f32[8,1024,128,3]{2,1,3,0:T(8,128)} %copy-done.2, f32[8,3,128]{2,1,0:T(4,128)S(1)} %broadcast_maximum_fusion, pred[128,1024]{0,1:T(8,128)(4,1)S(1)} %fusion.51, f32[128,8,3]{0,2,1:T(4,128)S(1)} %bitcast.233), kind=kOutput, calls=%fused_computation.49 | convolution fusion | flops 418775040 | bytes 14180352 | tf_op jit(solution)/shard_map/ukoe,euh->ukoh/dot_general | solution.py:132
  169.2 3.3 multiply_reduce_fusion
  172.7 11.9 %gather_fusion = bf16[3200,1536]{1,0:T(8,128)(2,1)} fusion(bf16[129,1536]{1,0:T(8,128)(2,1)S(1)} %concatenate.20, s32[4096]{0:T(1024)S(1)} %pad_clamp_fusion), kind=kCustom, calls=%fused_computation | custom fusion | bytes 19673600 | tf_op jit(solution)/shard_map/gather | solution.py:166
  184.5 117.5 %all_to_all.10 = bf16[16,5,40,1536]{3,2,1,0:T(8,128)(2,1)S(1)} all-to-all(bf16[16,5,40,1536]{3,2,1,0:T(8,128)(2,1)} %bitcast.208), channel_id=1, replica_groups=mesh['seq'=8,'grp'=16] {'grp'}, dimensions={0} | all-to-all | bytes 19660800 | tf_op jit(solution)/shard_map/all_to_all | solution.py:169
  302.1 3.8 copy-done.3
  305.8 4.6 fusion.6
  310.5 13.4 %fusion.1 = bf16[16,5,40,1536]{3,2,0,1:T(8,128)(2,1)} fusion(bf16[5,256,1536]{2,1,0:T(8,128)(2,1)} %param.35, f32[5,16,40,256]{3,2,1,0:T(8,128)} %fusion.6, bf16[5,1536,256]{2,1,0:T(8,128)(2,1)} %param.34, bf16[16,5,40,1536]{3,2,1,0:T(8,128)(2,1)} %copy-done.3), kind=kOutput, calls=%fused_computation.8 | convolution fusion | flops 5042995200 | bytes 30801920 | tf_op jit(solution)/shard_map/nlcf,lfd->nlcd/dot_general | solution.py:175
  323.9 8.3 %copy.70 = bf16[16,5,40,1536]{3,2,1,0:T(8,128)(2,1)} copy(bf16[16,5,40,1536]{3,2,0,1:T(8,128)(2,1)} %fusion.1) | data formatting | bytes 19660800 | tf_op jit(solution)/shard_map/convert_element_type | solution.py:177
  332.2 4.9 all-to-all-start.1
  338.2 141.3 %all-to-all-done.1 = bf16[16,5,40,1536]{3,2,1,0:T(8,128)(2,1)} async-done(((bf16[16,5,40,1536]{3,2,1,0:T(8,128)(2,1)}), bf16[16,5,40,1536]{3,2,1,0:T(8,128)(2,1)}, u32[]{:S(2)}, u32[]{:S(2)}) %all-to-all-start.1) | async-done | bytes 9830432 | tf_op jit(solution)/shard_map/all_to_all | solution.py:178
  479.5 18.3 %gather_fusion.1 = bf16[2048,1536]{1,0:T(8,128)(2,1)} fusion(bf16[3200,1536]{1,0:T(8,128)(2,1)} %bitcast.65, s32[2048]{0:T(1024)S(1)} %broadcast_clamp_fusion), kind=kCustom, calls=%fused_computation.1 | custom fusion | bytes 12591104 | tf_op jit(solution)/shard_map/gather | solution.py:183
  497.8 9.2 %convert_reduce_fusion = f32[128,1536]{1,0:T(8,128)S(1)} fusion(bf16[128,16,1536]{2,1,0:T(8,128)(2,1)} %bitcast.209, f32[128,16]{1,0:T(8,128)S(1)} %copy.62, s32[128,16]{1,0:T(8,128)S(1)} %copy.61), kind=kOutput, calls=%fused_computation.4 | convolution fusion | flops 613285888 | bytes 7094272 | tf_op jit(solution)/shard_map/tkg,tkd->tgd/dot_general | solution.py:189
  507.6 66.9 %all-reduce.2 = bf16[16,3,1536]{2,1,0:T(4,128)(2,1)S(1)} all-reduce(f32[16,3,1536]{2,1,0:T(4,128)S(1)} %broadcast_multiply_fusion), channel_id=1, replica_groups=mesh['seq'=8,'grp'=16] {'seq','grp'}, use_global_device_ids=true, to_apply=%region_15.16 | all-reduce | flops 73728 | bytes 442368 | tf_op jit(solution)/shard_map/psum | solution.py:200
  576.4 64.0 %pmax.7 = f32[48]{0:T(128)S(1)} all-reduce(f32[48]{0:T(128)S(1)} %get-tuple-element.22), channel_id=1, replica_groups=mesh['seq'=8,'grp'=16] {'seq','grp'}, use_global_device_ids=true, to_apply=%region_17.18 | all-reduce | flops 48 | bytes 384 | tf_op jit(solution)/shard_map/pmax | solution.py:203
  640.6 62.6 %psum.15 = f32[48]{0:T(128)S(1)} all-reduce(f32[48]{0:T(128)S(1)} %exponential_reduce_fusion), channel_id=1, replica_groups=mesh['seq'=8,'grp'=16] {'seq','grp'}, use_global_device_ids=true, to_apply=%region_19.20 | all-reduce | flops 48 | bytes 384 | tf_op jit(solution)/shard_map/psum | solution.py:204
  (110 shorter events, 36.2 us)
Async XLA Ops:
  7.2 58.4 %copy-start = (bf16[1536,512]{1,0:T(8,128)(2,1)S(1)}, bf16[1536,512]{1,0:T(8,128)(2,1)}, u32[]{:S(2)}) copy-start(bf16[1536,512]{1,0:T(8,128)(2,1)} %param.26) | copy-start | bytes 4718596
  7.2 57.7 %copy-start.4 = (bf16[1,128,1536]{2,1,0:T(8,128)(2,1)S(1)}, bf16[1,128,1536]{2,1,0:T(8,128)(2,1)}, u32[]{:S(2)}) copy-start(bf16[1,128,1536]{2,1,0:T(8,128)(2,1)} %param.19) | copy-start | bytes 1179652
  7.2 57.7 %copy-start.7 = (f32[1536]{0:T(1024)S(1)}, f32[1536]{0:T(1024)}, u32[]{:S(2)}) copy-start(f32[1536]{0:T(1024)} %param.24) | copy-start | bytes 18436
  7.2 54.5 %all-gather.5.cloned.1.call-start = ((), (), s32[]{:S(2)}) async-start(), calls=%async_computation.2 | async-start | bytes 3342336 | tf_op jit(solution)/shard_map/all_gather | solution.py:82
  7.9 98.1 %all-gather.9.cloned.1.call-start = ((), (), s32[]{:S(2)}) async-start(), calls=%async_computation.4 | async-start | bytes 1671168 | tf_op jit(solution)/shard_map/all_gather | solution.py:83
  8.7 122.9 %all-gather.7.cloned.1.call-start = ((), (), s32[]{:S(2)}) async-start(), calls=%async_computation.3 | async-start | bytes 1179648 | tf_op jit(solution)/shard_map/all_gather | solution.py:113
  68.5 89.7 %all-gather.11.cloned.1.call-start = ((), (), s32[]{:S(2)}) async-start(), calls=%async_computation.5 | async-start | bytes 1179648 | tf_op jit(solution)/shard_map/all_gather | solution.py:114
  134.8 4.6 copy-start.2
  160.5 8.4 %copy-start.5 = (bf16[2,16,16,1536]{3,2,1,0:T(8,128)(2,1)S(1)}, bf16[2,16,16,1536]{3,2,1,0:T(8,128)(2,1)}, u32[]{:S(2)}) copy-start(bf16[2,16,16,1536]{3,2,1,0:T(8,128)(2,1)} %all-gather.9.cloned.1.call-done) | copy-start | bytes 4718596
  168.5 4.0 copy-start.8
  184.5 121.3 %copy-start.11 = (bf16[5,1536,256]{2,1,0:T(8,128)(2,1)S(1)}, bf16[5,1536,256]{2,1,0:T(8,128)(2,1)}, u32[]{:S(2)}) copy-start(bf16[5,1536,256]{2,1,0:T(8,128)(2,1)} %param.33) | copy-start | bytes 11796484
  302.1 3.8 copy-start.3
  332.2 5.8 copy-start.10
  332.2 147.3 %all-to-all-start.1 = ((bf16[16,5,40,1536]{3,2,1,0:T(8,128)(2,1)}), bf16[16,5,40,1536]{3,2,1,0:T(8,128)(2,1)}, u32[]{:S(2)}, u32[]{:S(2)}) async-start(bf16[16,5,40,1536]{3,2,1,0:T(8,128)(2,1)} %copy.70), calls=%async_computation.1 | async-start | bytes 19660800 | tf_op jit(solution)/shard_map/all_to_all | solution.py:178
  497.8 206.1 %copy-start.1 = (bf16[1536,512]{1,0:T(8,128)(2,1)S(1)}, bf16[1536,512]{1,0:T(8,128)(2,1)}, u32[]{:S(2)}) copy-start(bf16[1536,512]{1,0:T(8,128)(2,1)} %param.26) | copy-start | bytes 4718596
  497.8 9.6 %copy-start.9 = (f32[1536]{0:T(1024)S(1)}, f32[1536]{0:T(1024)}, u32[]{:S(2)}) copy-start(f32[1536]{0:T(1024)} %param.36) | copy-start | bytes 18436
  507.1 196.8 %copy-start.6 = (bf16[128,1536]{1,0:T(8,128)(2,1)}, bf16[128,1536]{1,0:T(8,128)(2,1)S(1)}, u32[]{:S(2)}) copy-start(bf16[128,1536]{1,0:T(8,128)(2,1)S(1)} %add_convert_fusion) | copy-start | bytes 1179652
Sparse Core Ops, SparseCore 0:
  10.2 51.4 all-gather.4
  63.8 42.1 all-gather.8
  107.7 23.8 all-gather.6
  133.8 24.3 all-gather.10
where the time goes:
time: 712 us; the launch traced here: 710 us
  blocking collectives  333 us (47%)
  waiting for transfers between devices  219 us (31%)
  local copies, waits for them, and re-layouts  60.3 us (8%)
  matrix products  56.6 us (8%)
  other arithmetic  21.7 us (3%)
  between operations  14.3 us (2%)
    all_to_all x1, waiting for transfers between devices, body(): lax.all_to_all(halves, 'grp', split_axis=0, concat_axis=0, tiled=True)  141 us
    all_to_all x1, blocking collectives, body(): lax.all_to_all(outgoing, 'grp', split_axis=0, concat_axis=0, tiled=True)  118 us
    psum x1, blocking collectives, body(): gathered = lax.psum(spread, ('seq', 'grp'))  66.9 us
    pmax x1, blocking collectives, body(): global_max = lax.pmax(jnp.max(logits, axis=1), ('seq', 'grp'))  64 us
    psum x1, blocking collectives, body(): lax.psum(jnp.sum(jnp.exp(logits - global_max[:, None]), axis=1), ('seq',...  62.6 us
    all_gather x1, waiting for transfers between devices, body(): lax.all_gather(adapter_up_query_output, 'grp', axis=1, tiled=True)  35.7 us
    all_gather x1, blocking collectives, body(): lax.all_gather(adapter_up_key_value, 'grp', axis=1, tiled=True)  22.3 us
    gather x1, local copies, waits for them, and re-layouts, body(): returned[pick_index].astype(jnp.float32)  18.3 us
  transfers between devices with their start and end apart: 5, of which 5 were waited for; matrix products, arithmetic and copies ran while one was open for 7% of the time, Pallas kernels for 0%

commit v1 on v0

--- a/solution.py
+++ b/solution.py
@@ -111,7 +111,9 @@
     ).astype(jnp.bfloat16)
     running_max = jnp.full((KV_HEADS, ratio, tok_count), MASKED, jnp.float32)
     key_part = lax.all_gather(key_matrix, "seq", axis=0, tiled=True)
-    value_part = lax.all_gather(value_matrix, "seq", axis=0, tiled=True)
+    value_part = jnp.concatenate(
+        lax.all_to_all(jnp.stack([value_matrix] * lax.axis_size("seq")), "seq", 0, 0), axis=0
+    )
     key_count = key_part.shape[0]
     key_index = jnp.arange(key_count, dtype=jnp.int32)
     key_doc, _, _ = doc_layout(prompt_lens, key_index)

time: 712 us -> 683 us (0.959)
  waiting for transfers between devices: 219 us -> 193 us
  matrix products: 56.6 us -> 47.8 us
    all_gather x1 -> x0, waiting for transfers between devices: 15.8 us -> none  [body(): value_part = lax.all_gather(value_matrix, 'seq', axis=0, tiled=True)]
    all_gather x1, waiting for transfers between devices: 35.7 us -> 26.2 us  [body(): lax.all_gather(adapter_up_query_output, 'grp', axis=1, tiled=True)]
  transfers between devices with their start and end apart: 5 -> 5, of which waited for: 5 -> 4; matrix products, arithmetic and copies ran while one was open for 7% -> 7% of each run, Pallas kernels for 0% -> 0%
where the time goes in v1:
time: 683 us; the launch traced here: 682 us
  blocking collectives  334 us (49%)
  waiting for transfers between devices  193 us (28%)
  local copies, waits for them, and re-layouts  57.1 us (8%)
  matrix products  47.8 us (7%)
  other arithmetic  25.1 us (4%)
  between operations  14.4 us (2%)
  starting transfers between devices  10.6 us (2%)
    all_to_all x1, waiting for transfers between devices, body(): lax.all_to_all(halves, 'grp', split_axis=0, concat_axis=0, tiled=True)  141 us
    all_to_all x1, blocking collectives, body(): lax.all_to_all(outgoing, 'grp', split_axis=0, concat_axis=0, tiled=True)  118 us
    psum x1, blocking collectives, body(): gathered = lax.psum(spread, ('seq', 'grp'))  68.2 us
    psum x1, blocking collectives, body(): lax.psum(jnp.sum(jnp.exp(logits - global_max[:, None]), axis=1), ('seq',...  64 us
    pmax x1, blocking collectives, body(): global_max = lax.pmax(jnp.max(logits, axis=1), ('seq', 'grp'))  62.5 us
    all_gather x1, waiting for transfers between devices, body(): lax.all_gather(adapter_up_query_output, 'grp', axis=1, tiled=True)  26.2 us
    all_gather x1, blocking collectives, body(): lax.all_gather(adapter_up_key_value, 'grp', axis=1, tiled=True)  22.2 us
    all_gather x1, waiting for transfers between devices, body(): key_part = lax.all_gather(key_matrix, 'seq', axis=0, tiled=True)  18.6 us
  transfers between devices with their start and end apart: 5, of which 4 were waited for; matrix products, arithmetic and copies ran while one was open for 7% of the time, Pallas kernels for 0%

profile of v1, /device:TPU:1, one launch (start us, length us, event | category | flops | bytes accessed | tf_op | source)
XLA Modules:
  0.0 682.3 jit_solution(6585196381711706534)
XLA Ops:
  12.7 22.2 %all_gather.13 = bf16[2,16,16,512]{3,2,1,0:T(8,128)(2,1)S(1)} all-gather(bf16[2,1,16,512]{3,2,1,0:T(8,128)(2,1)} %param.31), channel_id=1, replica_groups=mesh['seq'=8,'grp'=16] {'grp'}, dimensions={1}, use_global_device_ids=true | all-gather | bytes 557056 | tf_op jit(solution)/shard_map/all_gather | solution.py:84
  34.9 11.3 %reduce-window.11 = s32[40,8,128]{2,1,0:T(8,128)S(1)} reduce-window(s32[40,8,128]{2,1,0:T(8,128)S(1)} %fusion.65, s32[]{:T(128)} %constant.32.clone.1), window={size=1x1x128 pad=0_0x0_0x127_0}, to_apply=%region_9.10 | reduce-window | flops 5201920 | bytes 327684 | tf_op jit(solution)/shard_map/reduce-window.1
  47.5 4.3 scatter_custom_fusion
  56.2 5.6 all-gather.4.cloned.1.call-done
  61.8 3.2 fusion.98
  74.0 5.4 all-to-all-start
  79.9 26.2 %all-gather.8.cloned.1.call-done = bf16[2,16,16,1536]{3,2,1,0:T(8,128)(2,1)} async-done(((bf16[2,1,16,1536]{3,2,1,0:T(8,128)(2,1)}), bf16[2,16,16,1536]{3,2,1,0:T(8,128)(2,1)}) %all-gather.8.cloned.1.call-update) | async-done | bytes 1572880 | tf_op jit(solution)/shard_map/all_gather | solution.py:83
  107.6 3.2 convolution_add_fusion.1
  113.2 18.6 %all-gather.6.cloned.1.call-done = bf16[1024,512]{0,1:T(8,128)(2,1)} async-done(((bf16[128,512]{0,1:T(8,128)(2,1)}), bf16[1024,512]{0,1:T(8,128)(2,1)}) %all-gather.6.cloned.1.call-update) | async-done | bytes 1048592 | tf_op jit(solution)/shard_map/all_gather | solution.py:113
  131.8 3.1 fusion
  138.0 3.5 fusion.43
  143.4 11.9 %gather_fusion = bf16[3200,1536]{1,0:T(8,128)(2,1)} fusion(bf16[129,1536]{1,0:T(8,128)(2,1)S(1)} %concatenate.20, s32[4096]{0:T(1024)S(1)} %pad_clamp_fusion), kind=kCustom, calls=%fused_computation | custom fusion | bytes 19673600 | tf_op jit(solution)/shard_map/gather | solution.py:168
  155.2 117.5 %all_to_all.15 = bf16[16,5,40,1536]{3,2,1,0:T(8,128)(2,1)S(1)} all-to-all(bf16[16,5,40,1536]{3,2,1,0:T(8,128)(2,1)} %bitcast.211), channel_id=1, replica_groups=mesh['seq'=8,'grp'=16] {'grp'}, dimensions={0} | all-to-all | bytes 19660800 | tf_op jit(solution)/shard_map/all_to_all | solution.py:171
  272.8 3.8 copy-done.2
  276.6 4.6 fusion.6
  281.2 13.4 %fusion.1 = bf16[16,5,40,1536]{3,2,0,1:T(8,128)(2,1)} fusion(bf16[5,256,1536]{2,1,0:T(8,128)(2,1)} %param.35, f32[5,16,40,256]{3,2,1,0:T(8,128)} %fusion.6, bf16[5,1536,256]{2,1,0:T(8,128)(2,1)} %param.34, bf16[16,5,40,1536]{3,2,1,0:T(8,128)(2,1)} %copy-done.2), kind=kOutput, calls=%fused_computation.8 | convolution fusion | flops 5042995200 | bytes 30801920 | tf_op jit(solution)/shard_map/nlcf,lfd->nlcd/dot_general | solution.py:177
  294.6 8.3 %copy.72 = bf16[16,5,40,1536]{3,2,1,0:T(8,128)(2,1)} copy(bf16[16,5,40,1536]{3,2,0,1:T(8,128)(2,1)} %fusion.1) | data formatting | bytes 19660800 | tf_op jit(solution)/shard_map/convert_element_type | solution.py:179
  302.9 5.1 all-to-all-start.2
  309.1 141.1 %all-to-all-done.2 = bf16[16,5,40,1536]{3,2,1,0:T(8,128)(2,1)} async-done(((bf16[16,5,40,1536]{3,2,1,0:T(8,128)(2,1)}), bf16[16,5,40,1536]{3,2,1,0:T(8,128)(2,1)}, u32[]{:S(2)}, u32[]{:S(2)}) %all-to-all-start.2) | async-done | bytes 9830432 | tf_op jit(solution)/shard_map/all_to_all | solution.py:180
  450.1 18.3 %gather_fusion.1 = bf16[2048,1536]{1,0:T(8,128)(2,1)} fusion(bf16[3200,1536]{1,0:T(8,128)(2,1)} %bitcast.63, s32[2048]{0:T(1024)S(1)} %broadcast_clamp_fusion), kind=kCustom, calls=%fused_computation.1 | custom fusion | bytes 12591104 | tf_op jit(solution)/shard_map/gather | solution.py:185
  468.5 9.2 %convert_reduce_fusion = f32[128,1536]{1,0:T(8,128)S(1)} fusion(bf16[128,16,1536]{2,1,0:T(8,128)(2,1)} %bitcast.212, f32[128,16]{1,0:T(8,128)S(1)} %copy.64, s32[128,16]{1,0:T(8,128)S(1)} %copy.63), kind=kOutput, calls=%fused_computation.4 | convolution fusion | flops 613285888 | bytes 7094272 | tf_op jit(solution)/shard_map/tkg,tkd->tgd/dot_general | solution.py:191
  478.3 68.2 %all-reduce.2 = bf16[16,3,1536]{2,1,0:T(4,128)(2,1)S(1)} all-reduce(f32[16,3,1536]{2,1,0:T(4,128)S(1)} %broadcast_multiply_fusion), channel_id=1, replica_groups=mesh['seq'=8,'grp'=16] {'seq','grp'}, use_global_device_ids=true, to_apply=%region_15.16 | all-reduce | flops 73728 | bytes 442368 | tf_op jit(solution)/shard_map/psum | solution.py:202
  548.3 62.5 %pmax.7 = f32[48]{0:T(128)S(1)} all-reduce(f32[48]{0:T(128)S(1)} %get-tuple-element.22), channel_id=1, replica_groups=mesh['seq'=8,'grp'=16] {'seq','grp'}, use_global_device_ids=true, to_apply=%region_17.18 | all-reduce | flops 48 | bytes 384 | tf_op jit(solution)/shard_map/pmax | solution.py:205
  611.1 64.0 %psum.15 = f32[48]{0:T(128)S(1)} all-reduce(f32[48]{0:T(128)S(1)} %exponential_reduce_fusion), channel_id=1, replica_groups=mesh['seq'=8,'grp'=16] {'seq','grp'}, use_global_device_ids=true, to_apply=%region_19.20 | all-reduce | flops 48 | bytes 384 | tf_op jit(solution)/shard_map/psum | solution.py:206
  (147 shorter events, 33.4 us)
Async XLA Ops:
  7.2 58.5 %copy-start = (bf16[1536,512]{1,0:T(8,128)(2,1)S(1)}, bf16[1536,512]{1,0:T(8,128)(2,1)}, u32[]{:S(2)}) copy-start(bf16[1536,512]{1,0:T(8,128)(2,1)} %param.26) | copy-start | bytes 4718596
  7.2 57.8 %copy-start.3 = (bf16[1,128,1536]{2,1,0:T(8,128)(2,1)S(1)}, bf16[1,128,1536]{2,1,0:T(8,128)(2,1)}, u32[]{:S(2)}) copy-start(bf16[1,128,1536]{2,1,0:T(8,128)(2,1)} %param.19) | copy-start | bytes 1179652
  7.2 57.8 %copy-start.11 = (f32[1536]{0:T(1024)S(1)}, f32[1536]{0:T(1024)}, u32[]{:S(2)}) copy-start(f32[1536]{0:T(1024)} %param.24) | copy-start | bytes 18436
  7.2 54.6 %all-gather.4.cloned.1.call-start = ((), (), s32[]{:S(2)}) async-start(), calls=%async_computation.3 | async-start | bytes 3342336 | tf_op jit(solution)/shard_map/all_gather | solution.py:82
  7.9 98.2 %all-gather.8.cloned.1.call-start = ((), (), s32[]{:S(2)}) async-start(), calls=%async_computation.5 | async-start | bytes 1671168 | tf_op jit(solution)/shard_map/all_gather | solution.py:83
  8.7 123.1 %all-gather.6.cloned.1.call-start = ((), (), s32[]{:S(2)}) async-start(), calls=%async_computation.4 | async-start | bytes 1179648 | tf_op jit(solution)/shard_map/all_gather | solution.py:113
  9.7 46.5 %copy-start.14 = (s32[1024]{0:T(1024)}, s32[1024]{0:T(1024)S(1)}, u32[]{:S(2)}) copy-start(s32[1024]{0:T(1024)S(1)} %broadcast_in_dim_reshape_squeeze.2) | copy-start | bytes 12292
  11.0 45.2 %copy-start.22 = (s32[128]{0:T(128)}, s32[128]{0:T(128)S(1)}, u32[]{:S(2)}) copy-start(s32[128]{0:T(128)S(1)} %iota_add_fusion) | copy-start | bytes 1540
  11.8 34.6 %copy-start.24 = (s32[3,1]{0,1:T(1,128)}, s32[3,1]{0,1:T(1,128)S(1)}, u32[]{:S(2)}) copy-start(s32[3,1]{0,1:T(1,128)S(1)} %reduce-window.10) | copy-start | bytes 40
  54.6 10.9 %copy-start.19 = (f32[128]{0:T(128)}, f32[128]{0:T(128)S(1)}, u32[]{:S(2)}) copy-start(f32[128]{0:T(128)S(1)} %add_rsqrt_fusion.2) | copy-start | bytes 1540
  66.8 12.7 %copy-start.20 = (f32[128]{0:T(128)S(1)}, f32[128]{0:T(128)}, u32[]{:S(2)}) copy-start(f32[128]{0:T(128)} %copy-done.19) | copy-start | bytes 1540
  74.0 37.0 %copy-start.9 = (f32[128,32]{0,1:T(8,128)S(1)}, f32[128,32]{0,1:T(8,128)}, u32[]{:S(2)}) copy-start(f32[128,32]{0,1:T(8,128)} %get-tuple-element.14) | copy-start | bytes 49156
  74.0 37.0 %copy-start.10 = (f32[128,32]{0,1:T(8,128)S(1)}, f32[128,32]{0,1:T(8,128)}, u32[]{:S(2)}) copy-start(f32[128,32]{0,1:T(8,128)} %get-tuple-element.15) | copy-start | bytes 49156
  74.0 37.1 %all-to-all-start = ((bf16[8,128,512]{1,2,0:T(8,128)(2,1)}), bf16[8,128,512]{1,2,0:T(8,128)(2,1)S(1)}, u32[]{:S(2)}, u32[]{:S(2)}) async-start(bf16[8,128,512]{1,2,0:T(8,128)(2,1)} %stack.2), calls=%async_computation | async-start | bytes 2097152 | tf_op jit(solution)/shard_map/all_to_all | solution.py:115
  107.6 24.2 %copy-start.7 = (pred[128,1024]{0,1:T(8,128)(4,1)S(1)}, pred[128,1024]{0,1:T(8,128)(4,1)}, u32[]{:S(2)}) copy-start(pred[128,1024]{0,1:T(8,128)(4,1)} %fusion.56) | copy-start | bytes 393220
  134.9 7.3 %slice-start = ((s8[4718592]{0:T(1024)(128)(4,1)}), s8[4194304]{0:T(1024)(128)(4,1)S(1)}, s32[]{:S(2)}) async-start(s8[4718592]{0:T(1024)(128)(4,1)} %bitcast.213), calls=%async_computation.6 | async-start | bytes 8388608
  155.2 121.3 %copy-start.26 = (bf16[5,1536,256]{2,1,0:T(8,128)(2,1)S(1)}, bf16[5,1536,256]{2,1,0:T(8,128)(2,1)}, u32[]{:S(2)}) copy-start(bf16[5,1536,256]{2,1,0:T(8,128)(2,1)} %param.33) | copy-start | bytes 11796484
  302.9 6.0 copy-start.21
  302.9 6.1 copy-start.25
  302.9 147.2 %all-to-all-start.2 = ((bf16[16,5,40,1536]{3,2,1,0:T(8,128)(2,1)}), bf16[16,5,40,1536]{3,2,1,0:T(8,128)(2,1)}, u32[]{:S(2)}, u32[]{:S(2)}) async-start(bf16[16,5,40,1536]{3,2,1,0:T(8,128)(2,1)} %copy.72), calls=%async_computation.2 | async-start | bytes 19660800 | tf_op jit(solution)/shard_map/all_to_all | solution.py:180
  468.5 207.3 %copy-start.1 = (bf16[1536,512]{1,0:T(8,128)(2,1)S(1)}, bf16[1536,512]{1,0:T(8,128)(2,1)}, u32[]{:S(2)}) copy-start(bf16[1536,512]{1,0:T(8,128)(2,1)} %param.26) | copy-start | bytes 4718596
  468.5 9.3 %copy-start.23 = (s32[128]{0:T(128)S(1)}, s32[128]{0:T(128)}, u32[]{:S(2)}) copy-start(s32[128]{0:T(128)} %copy-done.22) | copy-start | bytes 1540
  468.5 9.6 %copy-start.18 = (f32[1536]{0:T(1024)S(1)}, f32[1536]{0:T(1024)}, u32[]{:S(2)}) copy-start(f32[1536]{0:T(1024)} %param.36) | copy-start | bytes 18436
  477.8 198.0 %copy-start.6 = (bf16[128,1536]{1,0:T(8,128)(2,1)}, bf16[128,1536]{1,0:T(8,128)(2,1)S(1)}, u32[]{:S(2)}) copy-start(bf16[128,1536]{1,0:T(8,128)(2,1)S(1)} %add_convert_fusion) | copy-start | bytes 1179652
  (10 other events, 36.8 us)
Sparse Core Ops, SparseCore 0:
  10.2 51.5 all-gather.3
  63.9 42.1 all-gather.7
  107.8 23.8 all-gather.5
